TPU v7x, 256 devices: a whole 4x4x8 slice. The times are simulated.
256 devices in a mesh: seq: 32 (over x, y, core), head: 8 (over z).
Axes of the slice: x: 4, y: 4, z: 8, core: 2. Of those that a mesh axis runs over, the one named last changes fastest.
Arguments:
- new_states: bfloat16 [96, 1024], replicated, may hold values from -6 to 6
- lengths: int32 [24], replicated, may hold values from 1 to 16380, as said below
- cache_keys: bfloat16 [24, 16384, 1024], P(None, 'seq', 'head'), may hold values from -3000 to 3000
- cache_values: bfloat16 [24, 16384, 1024], P(None, 'seq', 'head'), may hold values from -6 to 6
- buckets: int32 [24, 4, 16384], P(None, None, 'seq'), may hold values from 0 to 31, as said below
- attn_gain: float32 [1024], replicated, may hold values from 0.25 to 1.75
- w_query: bfloat16 [1024, 1024], P(None, 'head'), may hold values from -0.0234375 to 0.0234375
- w_key: bfloat16 [1024, 1024], P(None, 'head'), may hold values from -0.1875 to 0.1875
- w_value: bfloat16 [1024, 1024], P(None, 'head'), may hold values from -0.1875 to 0.1875
- rel_bias: float32 [32, 16], P(None, 'head'), may hold values from -27 to 2
- w_out: bfloat16 [1024, 1024], P('head'), may hold values from -0.1875 to 0.1875
- ffn_gain: float32 [1024], replicated, may hold values from 0.25 to 1.75
- w_router: float32 [1024, 16], replicated, may hold values from -0.1875 to 0.1875
- w_gate: bfloat16 [16, 1024, 2816], P('head', None, 'seq'), may hold values from -0.1875 to 0.1875
- w_up: bfloat16 [16, 1024, 2816], P('head', None, 'seq'), may hold values from -0.1875 to 0.1875
- w_down: bfloat16 [16, 2816, 1024], P('head', 'seq'), may hold values from -0.109375 to 0.109375
- expert_picks: int32 [4, 24, 2], replicated, may hold values from 0 to 15, all different within a row; in each aligned block of 24 rows (0 to 23, 24 to 47, ..., all dimensions but the last counted through in order) at most 4 rows name the same one
- final_gain: float32 [1024], replicated, may hold values from 0.25 to 1.75
- w_vocab: bfloat16 [1024, 32128], P(None, 'seq'), may hold values from -0.5 to 0.5
Outputs:
- final_hidden: bfloat16 [96, 1024], P('head')
- hidden_norm: float32 [96], P('head')
- logit_max: float32 [96], P('head')
Inputs may be any that keep to these rules, and one draw needn't show every extreme that they name: `lengths`: some request has exactly 16380 cached positions. buckets[r, t, p] is the T5 relative position bucket (16 exact buckets, then logarithmic up to a distance of 128) of the distance lengths[r] + t - p where that is not negative, else 0. `expert_picks`: A request's two picks at a step differ; at each step no expert is picked by more than 4 requests, a bound that some block reaches.
All inputs are finite; a program needn't handle non-finite values.
Results may differ from a plain program's by a relative error of at most 0.0096.
Values may be sent and summed in bfloat16 or wider, within the bound.
A program may use at most 64 MiB of HBM per device.

v0:
```python
import jax
import jax.numpy as jnp
from jax import lax
from jax.sharding import PartitionSpec as P

CAP = 4


def joined(part, axis, combine):
    gathered = jax.tree.map(lambda a: lax.all_gather(a, axis), part)

    def take(source):
        return jax.tree.map(lambda a: lax.dynamic_index_in_dim(a, source, 0, False), gathered)

    return lax.fori_loop(
        1, lax.axis_size(axis), lambda source, state: combine(state, take(source)), take(0)
    )


def norm_parts(values, gain_row):
    norm_root = jnp.sqrt(jnp.mean(values * values, axis=-1, keepdims=True) + 1e-06)
    return (values / norm_root * gain_row, norm_root[..., 0])


def join_three(earlier_part, later_part):
    joint_top = jnp.maximum(earlier_part[0], later_part[0])
    lead_scale = jnp.exp(earlier_part[0] - joint_top)
    trail_scale = jnp.exp(later_part[0] - joint_top)
    mass = earlier_part[1] * lead_scale + later_part[1] * trail_scale
    weighted = earlier_part[2] * lead_scale[..., None] + later_part[2] * trail_scale[..., None]
    return (joint_top, mass, weighted)


def shards(
    new_states,
    lengths,
    cache_keys,
    cache_values,
    buckets,
    attn_gain,
    w_query,
    w_key,
    w_value,
    rel_bias,
    w_out,
    ffn_gain,
    w_router,
    w_gate,
    w_up,
    w_down,
    expert_picks,
    final_gain,
    w_vocab,
):
    seq_count = lax.axis_size("seq")
    head_count = lax.axis_size("head")
    seq_index = lax.axis_index("seq")
    head_index = lax.axis_index("head")
    requests, span_local, inner_local = cache_keys.shape
    tokens = new_states.shape[0]
    step_count = tokens // requests
    bucket_count, heads_local = rel_bias.shape
    head_dim = inner_local // heads_local
    states = new_states.astype(jnp.float32)
    scaled, _ = norm_parts(states, attn_gain)
    scaled = scaled.astype(jnp.bfloat16)
    queries = (
        jnp.dot(scaled, w_query, preferred_element_type=jnp.float32)
        .astype(jnp.bfloat16)
        .reshape(requests, step_count, heads_local, head_dim)
    )
    key_new = (
        jnp.dot(scaled, w_key, preferred_element_type=jnp.float32)
        .astype(jnp.bfloat16)
        .reshape(requests, step_count, inner_local)
    )
    value_new = (
        jnp.dot(scaled, w_value, preferred_element_type=jnp.float32)
        .astype(jnp.bfloat16)
        .reshape(requests, step_count, inner_local)
    )
    position = seq_index * span_local + jnp.arange(span_local, dtype=jnp.int32)
    target = lengths[:, None] + jnp.arange(step_count, dtype=jnp.int32)[None, :]
    landing = position[None, None, :] == target[:, :, None]
    landed = jnp.any(landing, axis=1)[:, :, None]
    landing_low = landing.astype(jnp.bfloat16)
    placed_keys = jnp.einsum(
        "rtp,rtc->rpc", landing_low, key_new, preferred_element_type=jnp.float32
    ).astype(jnp.bfloat16)
    placed_values = jnp.einsum(
        "rtp,rtc->rpc", landing_low, value_new, preferred_element_type=jnp.float32
    ).astype(jnp.bfloat16)
    key_rows = jnp.where(landed, placed_keys, cache_keys).reshape(
        requests, span_local, heads_local, head_dim
    )
    value_rows = jnp.where(landed, placed_values, cache_values).reshape(
        requests, span_local, heads_local, head_dim
    )
    scores = jnp.einsum("rthd,rphd->rthp", queries, key_rows, preferred_element_type=jnp.float32)
    bucket_hot = (buckets[..., None] == jnp.arange(bucket_count, dtype=jnp.int32)).astype(
        jnp.float32
    )
    scores = scores + jnp.einsum(
        "rtpb,bh->rthp", bucket_hot, rel_bias, precision=lax.Precision.HIGHEST
    )
    allowed = (position[None, None, :] <= target[:, :, None])[:, :, None, :]
    scores = jnp.where(allowed, scores, -1e30)
    local_top = jnp.max(scores, axis=-1)
    weights = jnp.where(allowed, jnp.exp(scores - local_top[..., None]), 0.0)
    local_mass = jnp.sum(weights, axis=-1)
    partial_value = jnp.einsum(
        "rthp,rphd->rthd", weights, value_rows.astype(jnp.float32), precision=lax.Precision.HIGHEST
    )
    out_rows = w_out.astype(jnp.float32)
    global_top, global_mass, summed = joined(
        (local_top, local_mass, partial_value), "seq", join_three
    )
    heads_out = (summed / global_mass[..., None]).reshape(tokens, inner_local)
    projected = jnp.dot(heads_out, out_rows, precision=lax.Precision.HIGHEST)
    mixed_rows = lax.psum(projected, "head")
    hidden_one = states + mixed_rows
    normed, _ = norm_parts(hidden_one, ffn_gain)
    router_logits = jnp.dot(normed, w_router, precision=lax.Precision.HIGHEST)
    normed_low = normed.astype(jnp.bfloat16)
    expert_total = w_router.shape[1]
    local_experts, model_width, units_local = w_gate.shape
    expert_ids = jnp.arange(expert_total, dtype=jnp.int32)
    pick_marks = (expert_picks[..., None] == expert_ids).astype(jnp.int32)
    per_step = jnp.sum(pick_marks, axis=2)
    earlier = jnp.cumsum(per_step, axis=1) - per_step
    slot_index = jnp.sum(pick_marks * earlier[:, :, None, :], axis=-1)
    pick_total = expert_picks.shape[2]
    token_picks = jnp.transpose(expert_picks, (1, 0, 2)).reshape(tokens, pick_total)
    token_slots = jnp.transpose(slot_index, (1, 0, 2)).reshape(tokens, pick_total)
    token_steps = jnp.arange(tokens, dtype=jnp.int32) % step_count
    picked = jnp.sum(
        jnp.where(token_picks[..., None] == expert_ids, router_logits[:, None, :], 0.0), axis=-1
    )
    gate_first = jax.nn.sigmoid(picked[:, 0] - picked[:, 1])
    gate_second = jax.nn.sigmoid(picked[:, 1] - picked[:, 0])
    slot_rows = step_count * CAP
    row_ids = jnp.arange(local_experts * slot_rows, dtype=jnp.int32)
    row_expert = head_index * local_experts + row_ids // slot_rows
    row_step = row_ids // CAP % step_count
    row_slot = row_ids % CAP
    chooser = jnp.zeros((row_ids.shape[0], tokens), jnp.float32)
    for pick_rank in range(pick_total):
        matched = (
            (row_expert[:, None] == token_picks[None, :, pick_rank])
            & (row_step[:, None] == token_steps[None, :])
            & (row_slot[:, None] == token_slots[None, :, pick_rank])
        )
        chooser = chooser + matched.astype(jnp.float32)
    routed = jnp.dot(
        chooser.astype(jnp.bfloat16), normed_low, preferred_element_type=jnp.float32
    ).astype(jnp.bfloat16)
    routed = routed.reshape(local_experts, slot_rows, model_width)
    gate_part = jnp.einsum("esd,edf->esf", routed, w_gate, preferred_element_type=jnp.float32)
    up_part = jnp.einsum("esd,edf->esf", routed, w_up, preferred_element_type=jnp.float32)
    hidden_units = (jax.nn.gelu(gate_part, approximate=True) * up_part).astype(jnp.bfloat16)
    down_part = jnp.einsum("esf,efd->esd", hidden_units, w_down, preferred_element_type=jnp.float32)
    expert_share = lax.psum_scatter(down_part, "seq", scatter_dimension=2, tiled=True).astype(
        jnp.bfloat16
    )
    share_width = expert_share.shape[2]
    collected = lax.all_gather(expert_share[None], ("seq", "head"), axis=0, tiled=True)
    arranged = collected.reshape(seq_count, head_count, local_experts, slot_rows, share_width)
    arranged = jnp.transpose(arranged, (1, 2, 3, 0, 4)).reshape(
        expert_total * slot_rows, seq_count * share_width
    )
    group_size = tokens // head_count
    first_row = head_index * group_size
    own_picks = lax.dynamic_slice_in_dim(token_picks, first_row, group_size, 0)
    own_slots = lax.dynamic_slice_in_dim(token_slots, first_row, group_size, 0)
    own_steps = lax.dynamic_slice_in_dim(token_steps, first_row, group_size, 0)
    own_first = lax.dynamic_slice_in_dim(gate_first, first_row, group_size, 0)
    own_second = lax.dynamic_slice_in_dim(gate_second, first_row, group_size, 0)
    own_hidden = lax.dynamic_slice_in_dim(hidden_one, first_row, group_size, 0)
    flat_rows = own_picks * slot_rows + own_steps[:, None] * CAP + own_slots
    every_row = jnp.arange(expert_total * slot_rows, dtype=jnp.int32)
    select_first = (flat_rows[:, 0:1] == every_row[None, :]).astype(jnp.bfloat16)
    select_second = (flat_rows[:, 1:2] == every_row[None, :]).astype(jnp.bfloat16)
    expert_mix = own_first[:, None] * jnp.dot(
        select_first, arranged, preferred_element_type=jnp.float32
    )
    expert_mix = expert_mix + own_second[:, None] * jnp.dot(
        select_second, arranged, preferred_element_type=jnp.float32
    )
    final_rows = (own_hidden + expert_mix).astype(jnp.bfloat16)
    scaled_out, norm_root = norm_parts(final_rows.astype(jnp.float32), final_gain)
    logits = jnp.dot(scaled_out.astype(jnp.bfloat16), w_vocab, preferred_element_type=jnp.float32)
    top_logit = lax.pmax(jnp.max(logits, axis=-1), "seq")
    return (final_rows, norm_root, top_logit)


def solution(mesh):
    placed = (
        P(),
        P(),
        P(None, "seq", "head"),
        P(None, "seq", "head"),
        P(None, None, "seq"),
        P(),
        P(None, "head"),
        P(None, "head"),
        P(None, "head"),
        P(None, "head"),
        P("head", None),
        P(),
        P(),
        P("head", None, "seq"),
        P("head", None, "seq"),
        P("head", "seq", None),
        P(),
        P(),
        P(None, "seq"),
    )
    return jax.shard_map(
        shards,
        mesh=mesh,
        in_specs=placed,
        out_specs=(P("head", None), P("head"), P("head")),
        check_vma=False,
    )
```

profile of v0, /device:TPU:32, one launch (start us, length us, event | category | flops | bytes accessed | tf_op | source)
XLA Modules:
  0.0 482.6 jit_solution(6117893066806250847)
XLA Ops:
  7.3 1.2 fusion.13
  9.2 1.3 convolution_convert_fusion.2
  10.7 1.3 convolution_convert_fusion.1
  12.3 4.6 copy.74
  17.0 4.7 copy.77
  22.0 2.0 fusion.4
  24.0 3.1 convert_select_fusion.1
  27.1 1.0 convert_select_fusion
  28.8 3.3 convolution_bitcast_fusion.1
  33.2 25.3 %all-gather.1 = f32[768,4,2]{1,2,0:T(2,128)S(1)} all-gather(f32[24,4,2]{1,2,0:T(2,128)S(1)} %fusion.16), channel_id=3, replica_groups=mesh['seq'=32,'head'=8] {'seq'}, dimensions={0}, use_global_device_ids=true | all-gather | bytes 25344 | tf_op jit(solution)/shard_map/all_gather | solution.py:10
  59.2 25.2 %all-gather = f32[768,4,2]{1,2,0:T(2,128)S(1)} all-gather(f32[24,4,2]{1,2,0:T(2,128)S(1)} %get-tuple-element.240), channel_id=2, replica_groups=mesh['seq'=32,'head'=8] {'seq'}, dimensions={0}, use_global_device_ids=true | all-gather | bytes 25344 | tf_op jit(solution)/shard_map/all_gather | solution.py:10
  84.4 1.2 copy.83
  87.0 76.0 %while.19 = (s32[]{:T(128)}, f32[24,4,2]{0,2,1:T(2,128)S(1)}, f32[24,4,2]{0,2,1:T(2,128)S(1)}, f32[24,4,2,64]{3,2,1,0:T(2,128)S(1)}, f32[32,24,4,2]{1,3,2,0:T(2,...) while((s32[]{:T(128)}, f32[24,4,2]{0,2,1:T(2,128)S(1)}, ...), condition=%wide.region_5.6_spmd, body=%wide.region_4.5_spmd.sunk | while | flops 38021 | bytes 256655 | solution.py:15
  87.9 0.9 constant_dynamic-slice_fusion.6
  90.4 0.9 constant_dynamic-slice_fusion.6
  92.8 0.9 constant_dynamic-slice_fusion.6
  95.3 0.9 constant_dynamic-slice_fusion.6
  97.7 0.9 constant_dynamic-slice_fusion.6
  100.2 0.9 constant_dynamic-slice_fusion.6
  102.6 0.9 constant_dynamic-slice_fusion.6
  105.1 0.9 constant_dynamic-slice_fusion.6
  107.6 0.9 constant_dynamic-slice_fusion.6
  110.0 0.9 constant_dynamic-slice_fusion.6
  112.5 0.9 constant_dynamic-slice_fusion.6
  114.9 0.9 constant_dynamic-slice_fusion.6
  117.4 0.9 constant_dynamic-slice_fusion.6
  119.8 0.9 constant_dynamic-slice_fusion.6
  122.3 0.9 constant_dynamic-slice_fusion.6
  124.7 0.9 constant_dynamic-slice_fusion.6
  127.2 0.9 constant_dynamic-slice_fusion.6
  129.6 0.9 constant_dynamic-slice_fusion.6
  132.1 0.9 constant_dynamic-slice_fusion.6
  134.5 0.9 constant_dynamic-slice_fusion.6
  137.0 0.9 constant_dynamic-slice_fusion.6
  151.7 0.9 constant_dynamic-slice_fusion.6
  156.6 0.9 constant_dynamic-slice_fusion.6
  163.4 1.1 fusion.77
  164.6 72.5 %all-reduce.2.cloned.1.call-done = f32[96,1024]{1,0:T(8,128)} async-done(((f32[96,1024]{1,0:T(8,128)}), f32[96,1024]{1,0:T(8,128)}) %all-reduce.2.cloned.1.call-update) | async-done | bytes 393232 | tf_op jit(solution)/shard_map/psum | solution.py:120
  237.1 1.1 multiply_reduce_fusion
  239.1 1.2 fusion.78
  240.3 2.0 fusion.12
  242.3 1.3 copy.98
  243.6 1.4 reshape.208
  245.2 83.7 %reduce-scatter.4.cloned.1.call-done = f32[32,32]{1,0:T(8,128)} async-done(((f32[1024,32]{1,0:T(8,128)}), f32[32,32]{1,0:T(8,128)}) %reduce-scatter.4.cloned.1.call-update) | async-done | bytes 4112
  329.8 73.4 %all-gather.3 = bf16[512,16,32]{2,1,0:T(8,128)(2,1)S(1)} all-gather(bf16[2,16,32]{2,1,0:T(8,128)(2,1)S(1)} %copy.99), channel_id=5, replica_groups=mesh['seq'=32,'head'=8] {'seq','head'}, dimensions={0}, use_global_device_ids=true | all-gather | bytes 526336 | tf_op jit(solution)/shard_map/all_gather | solution.py:166
  403.2 2.7 copy.112
  405.9 3.5 reshape.189
  410.8 65.3 %pmax.7 = f32[12]{0:T(128)} all-reduce(f32[12]{0:T(128)S(1)} %convolution_reduce_fusion), channel_id=1, replica_groups=mesh['seq'=32,'head'=8] {'seq'}, use_global_device_ids=true, to_apply=%region_15.16 | all-reduce | flops 12 | bytes 96 | tf_op jit(solution)/shard_map/pmax | solution.py:192
  (217 shorter events, 63.7 us)
Async XLA Ops:
  7.2 402.9 %copy-start = (bf16[1024,1004]{0,1:T(8,128)(2,1)S(1)}, bf16[1024,1004]{0,1:T(8,128)(2,1)}, u32[]{:S(2)}) copy-start(bf16[1024,1004]{0,1:T(8,128)(2,1)} %param.39) | copy-start | bytes 6168580
  7.2 4.8 copy-start.2
  7.2 4.8 copy-start.12
  7.2 4.8 copy-start.9
  7.2 78.8 %all-gather.6.cloned.1.call-start = ((), (), s32[]{:S(2)}) async-start(), calls=%async_computation.2 | async-start | bytes 3244032 | tf_op jit(solution)/shard_map/all_gather | solution.py:10
  16.9 5.0 %copy-start.10 = (s32[24,4,512]{2,1,0:T(4,128)S(1)}, s32[24,4,512]{2,1,0:T(4,128)}, u32[]{:S(2)}) copy-start(s32[24,4,512]{2,1,0:T(4,128)} %param.25) | copy-start | bytes 589828
  17.0 5.0 %copy-start.14 = (f32[32,2]{0,1:T(2,128)S(1)}, f32[32,2]{0,1:T(2,128)}, u32[]{:S(2)}) copy-start(f32[32,2]{0,1:T(2,128)} %param.30) | copy-start | bytes 772
  24.0 3.1 copy-start.1
  28.8 3.3 copy-start.6
  32.1 205.0 %all-reduce.2.cloned.1.call-start = ((), (), s32[]{:S(2)}) async-start(), calls=%async_computation.1 | async-start | bytes 786432 | tf_op jit(solution)/shard_map/psum | solution.py:120
  59.1 104.3 %copy-start.4 = (bf16[128,1024]{1,0:T(8,128)(2,1)S(1)}, bf16[128,1024]{1,0:T(8,128)(2,1)}, u32[]{:S(2)}) copy-start(bf16[128,1024]{1,0:T(8,128)(2,1)} %param.31) | copy-start | bytes 786436
  86.9 151.3 %copy-start.11 = (f32[1024,16]{0,1:T(8,128)S(1)}, f32[1024,16]{0,1:T(8,128)}, u32[]{:S(2)}) copy-start(f32[1024,16]{0,1:T(8,128)} %param.33) | copy-start | bytes 196612
  87.0 151.3 %copy-start.13 = (f32[1024]{0:T(1024)S(1)}, f32[1024]{0:T(1024)}, u32[]{:S(2)}) copy-start(f32[1024]{0:T(1024)} %param.32) | copy-start | bytes 12292
  163.0 77.3 %copy-start.3 = (bf16[2,88,1024]{2,1,0:T(8,128)(2,1)S(1)}, bf16[2,88,1024]{2,1,0:T(8,128)(2,1)}, u32[]{:S(2)}) copy-start(bf16[2,88,1024]{2,1,0:T(8,128)(2,1)} %param.36) | copy-start | bytes 1081348
  164.5 164.3 %reduce-scatter.4.cloned.1.call-start = ((), (), s32[]{:S(2)}) async-start(), calls=%async_computation.3 | async-start | bytes 540672
  403.2 6.8 %copy-start.7 = (f32[1024]{0:T(1024)S(1)}, f32[1024]{0:T(1024)}, u32[]{:S(2)}) copy-start(f32[1024]{0:T(1024)} %param.38) | copy-start | bytes 12292
  410.0 66.1 %copy-start.5 = (bf16[12,1024]{1,0:T(8,128)(2,1)}, bf16[12,1024]{1,0:T(8,128)(2,1)S(1)}, u32[]{:S(2)}) copy-start(bf16[12,1024]{1,0:T(8,128)(2,1)S(1)} %get-tuple-element.243) | copy-start | bytes 73732
  410.0 66.1 %copy-start.8 = (f32[12]{0:T(128)}, f32[12]{0:T(128)S(1)}, u32[]{:S(2)}) copy-start(f32[12]{0:T(128)S(1)} %add_sqrt_fusion) | copy-start | bytes 148
Sparse Core Ops, SparseCore 0:
  32.2 53.7 all-gather.5
  164.6 72.4 all-reduce.1
  245.2 83.6 reduce-scatter.3
where the time goes:
time: 485 us; the launch traced here: 483 us
  blocking collectives  189 us (39%)
  waiting for transfers between devices  156 us (32%)
  local copies, waits for them, and re-layouts  58.1 us (12%)
  other arithmetic  44.9 us (9%)
  matrix products  19.3 us (4%)
  between operations  14.1 us (3%)
    unnamed x4, waiting for transfers between devices  83.7 us
    all_gather x1, blocking collectives, shards(): lax.all_gather(expert_share[None], ('seq', 'head'), axis=0, tiled=True)  73.4 us
    psum x1, waiting for transfers between devices, shards(): mixed_rows = lax.psum(projected, 'head')  72.5 us
    pmax x1, blocking collectives, shards(): top_logit = lax.pmax(jnp.max(logits, axis=-1), 'seq')  65.3 us
    all_gather x2, blocking collectives, joined(): gathered = jax.tree.map(lambda a: lax.all_gather(a, axis), part)  50.5 us
    dynamic_slice x34, local copies, waits for them, and re-layouts, take(): lax.dynamic_index_in_dim(a, source, 0, False)  28.9 us
    add x31, other arithmetic, join_three(): mass = earlier_part[1] * lead_scale + later_part[1] * trail_scale  21.9 us
    add x31, other arithmetic, join_three(): earlier_part[2] * lead_scale[..., None]  18.8 us
  transfers between devices with their start and end apart: 3, of which 3 were waited for; matrix products, arithmetic and copies ran while one was open for 1% of the time, Pallas kernels for 0%

commit v1 on v0

--- a/solution.py
+++ b/solution.py
@@ -117,7 +117,8 @@
     )
     heads_out = (summed / global_mass[..., None]).reshape(tokens, inner_local)
     projected = jnp.dot(heads_out, out_rows, precision=lax.Precision.HIGHEST)
-    mixed_rows = lax.psum(projected, "head")
+    shards_2 = lax.all_gather(projected, "head", axis=0, tiled=False)
+    mixed_rows = shards_2.sum(axis=0)
     hidden_one = states + mixed_rows
     normed, _ = norm_parts(hidden_one, ffn_gain)
     router_logits = jnp.dot(normed, w_router, precision=lax.Precision.HIGHEST)

time: 485 us -> 458 us (0.944)
  waiting for transfers between devices: 156 us -> 128 us
    psum x1 -> x0, waiting for transfers between devices: 72.5 us -> none  [shards(): mixed_rows = lax.psum(projected, 'head')]
    all_gather x0 -> x1, waiting for transfers between devices: none -> 42.8 us  [shards(): shards_2 = lax.all_gather(projected, 'head', axis=0, tiled=False)]
where the time goes in v1:
time: 458 us; the launch traced here: 455 us
  blocking collectives  189 us (41%)
  waiting for transfers between devices  128 us (28%)
  local copies, waits for them, and re-layouts  58.1 us (13%)
  other arithmetic  46.1 us (10%)
  matrix products  19.1 us (4%)
  between operations  14.1 us (3%)
    unnamed x4, waiting for transfers between devices  84.3 us
    all_gather x1, blocking collectives, shards(): lax.all_gather(expert_share[None], ('seq', 'head'), axis=0, tiled=True)  73.4 us
    pmax x1, blocking collectives, shards(): top_logit = lax.pmax(jnp.max(logits, axis=-1), 'seq')  65.3 us
    all_gather x2, blocking collectives, joined(): gathered = jax.tree.map(lambda a: lax.all_gather(a, axis), part)  50.3 us
    all_gather x1, waiting for transfers between devices, shards(): shards_2 = lax.all_gather(projected, 'head', axis=0, tiled=False)  42.8 us
    dynamic_slice x34, local copies, waits for them, and re-layouts, take(): lax.dynamic_index_in_dim(a, source, 0, False)  28.9 us
    add x31, other arithmetic, join_three(): mass = earlier_part[1] * lead_scale + later_part[1] * trail_scale  21.9 us
    add x31, other arithmetic, join_three(): earlier_part[2] * lead_scale[..., None]  18.8 us
  transfers between devices with their start and end apart: 3, of which 3 were waited for; matrix products, arithmetic and copies ran while one was open for 1% of the time, Pallas kernels for 0%

profile of v1, /device:TPU:32, one launch (start us, length us, event | category | flops | bytes accessed | tf_op | source)
XLA Modules:
  0.0 455.0 jit_solution(17341566296934083669)
XLA Ops:
  7.3 1.2 fusion.13
  9.2 1.3 convolution_convert_fusion.2
  10.7 1.3 convolution_convert_fusion.1
  12.3 4.6 %copy.74 = bf16[24,512,128]{1,2,0:T(8,128)(2,1)} copy(bf16[24,512,128]{2,1,0:T(8,128)(2,1)} %param.23) | data formatting | bytes 6291456 | tf_op args[2]
  17.0 4.7 %copy.77 = bf16[24,512,128]{1,2,0:T(8,128)(2,1)} copy(bf16[24,512,128]{2,1,0:T(8,128)(2,1)} %param.24) | data formatting | bytes 6291456 | tf_op args[3]
  22.0 2.0 fusion.4
  24.0 3.1 convert_select_fusion.1
  27.1 1.0 convert_select_fusion
  28.8 3.3 convolution_bitcast_fusion.1
  32.5 25.2 %all-gather.1 = f32[768,4,2]{1,2,0:T(2,128)S(1)} all-gather(f32[24,4,2]{1,2,0:T(2,128)S(1)} %fusion.16), channel_id=3, replica_groups=mesh['seq'=32,'head'=8] {'seq'}, dimensions={0}, use_global_device_ids=true | all-gather | bytes 25344 | tf_op jit(solution)/shard_map/all_gather | solution.py:10
  58.4 25.1 %all-gather = f32[768,4,2]{1,2,0:T(2,128)S(1)} all-gather(f32[24,4,2]{1,2,0:T(2,128)S(1)} %get-tuple-element.240), channel_id=2, replica_groups=mesh['seq'=32,'head'=8] {'seq'}, dimensions={0}, use_global_device_ids=true | all-gather | bytes 25344 | tf_op jit(solution)/shard_map/all_gather | solution.py:10
  83.6 1.2 copy.83
  86.6 76.0 %while.19 = (s32[]{:T(128)}, f32[24,4,2]{0,2,1:T(2,128)S(1)}, f32[24,4,2]{0,2,1:T(2,128)S(1)}, f32[24,4,2,64]{3,2,1,0:T(2,128)S(1)}, f32[32,24,4,2]{1,3,2,0:T(2,...) while((s32[]{:T(128)}, f32[24,4,2]{0,2,1:T(2,128)S(1)}, ...), condition=%wide.region_5.6_spmd, body=%wide.region_4.5_spmd.sunk | while | flops 38021 | bytes 256655 | solution.py:15
  87.5 0.9 constant_dynamic-slice_fusion.6
  90.0 0.9 constant_dynamic-slice_fusion.6
  92.4 0.9 constant_dynamic-slice_fusion.6
  94.9 0.9 constant_dynamic-slice_fusion.6
  97.3 0.9 constant_dynamic-slice_fusion.6
  99.8 0.9 constant_dynamic-slice_fusion.6
  102.3 0.9 constant_dynamic-slice_fusion.6
  104.7 0.9 constant_dynamic-slice_fusion.6
  107.2 0.9 constant_dynamic-slice_fusion.6
  109.6 0.9 constant_dynamic-slice_fusion.6
  112.1 0.9 constant_dynamic-slice_fusion.6
  114.5 0.9 constant_dynamic-slice_fusion.6
  117.0 0.9 constant_dynamic-slice_fusion.6
  119.5 0.9 constant_dynamic-slice_fusion.6
  121.9 0.9 constant_dynamic-slice_fusion.6
  124.4 0.9 constant_dynamic-slice_fusion.6
  126.8 0.9 constant_dynamic-slice_fusion.6
  129.3 0.9 constant_dynamic-slice_fusion.6
  131.7 0.9 constant_dynamic-slice_fusion.6
  136.6 0.9 constant_dynamic-slice_fusion.6
  141.5 0.9 constant_dynamic-slice_fusion.6
  144.0 0.9 constant_dynamic-slice_fusion.6
  148.9 0.9 constant_dynamic-slice_fusion.6
  163.1 1.1 fusion.77
  165.1 42.8 %all-gather.10.cloned.1.call-done = f32[768,1024]{1,0:T(8,128)} async-done(((f32[96,1024]{1,0:T(8,128)}), f32[768,1024]{1,0:T(8,128)}) %all-gather.10.cloned.1.call-update) | async-done | bytes 3145744 | tf_op jit(solution)/shard_map/all_gather | solution.py:120
  207.9 2.2 reduce_sum.74
  210.2 1.3 fusion.31
  212.1 2.0 fusion.12
  214.1 1.3 copy.98
  215.4 1.4 reshape.209
  217.0 84.2 %reduce-scatter.4.cloned.1.call-done = f32[32,32]{1,0:T(8,128)} async-done(((f32[1024,32]{1,0:T(8,128)}), f32[32,32]{1,0:T(8,128)}) %reduce-scatter.4.cloned.1.call-update) | async-done | bytes 4112
  302.1 73.4 %all-gather.4 = bf16[512,16,32]{2,1,0:T(8,128)(2,1)S(1)} all-gather(bf16[2,16,32]{2,1,0:T(8,128)(2,1)S(1)} %copy.99), channel_id=6, replica_groups=mesh['seq'=32,'head'=8] {'seq','head'}, dimensions={0}, use_global_device_ids=true | all-gather | bytes 526336 | tf_op jit(solution)/shard_map/all_gather | solution.py:167
  375.6 2.7 copy.112
  378.3 3.5 reshape.189
  383.2 65.3 %pmax.7 = f32[12]{0:T(128)} all-reduce(f32[12]{0:T(128)S(1)} %convolution_reduce_fusion), channel_id=1, replica_groups=mesh['seq'=32,'head'=8] {'seq'}, use_global_device_ids=true, to_apply=%region_15.16 | all-reduce | flops 12 | bytes 96 | tf_op jit(solution)/shard_map/pmax | solution.py:193
  (218 shorter events, 64.2 us)
Async XLA Ops:
  7.2 375.2 %copy-start = (bf16[1024,1004]{0,1:T(8,128)(2,1)S(1)}, bf16[1024,1004]{0,1:T(8,128)(2,1)}, u32[]{:S(2)}) copy-start(bf16[1024,1004]{0,1:T(8,128)(2,1)} %param.39) | copy-start | bytes 6168580
  7.2 4.8 %copy-start.2 = (bf16[96,1024]{1,0:T(8,128)(2,1)S(1)}, bf16[96,1024]{1,0:T(8,128)(2,1)}, u32[]{:S(2)}) copy-start(bf16[96,1024]{1,0:T(8,128)(2,1)} %param.21) | copy-start | bytes 589828
  7.2 4.8 %copy-start.12 = (f32[1024]{0:T(1024)S(1)}, f32[1024]{0:T(1024)}, u32[]{:S(2)}) copy-start(f32[1024]{0:T(1024)} %param.26) | copy-start | bytes 12292
  7.2 4.8 %copy-start.10 = (bf16[1024,128]{1,0:T(8,128)(2,1)S(1)}, bf16[1024,128]{1,0:T(8,128)(2,1)}, u32[]{:S(2)}) copy-start(bf16[1024,128]{1,0:T(8,128)(2,1)} %param.28) | copy-start | bytes 786436
  7.2 78.4 %all-gather.8.cloned.1.call-start = ((), (), s32[]{:S(2)}) async-start(), calls=%async_computation.1 | async-start | bytes 3244032 | tf_op jit(solution)/shard_map/all_gather | solution.py:10
  16.9 5.0 %copy-start.11 = (s32[24,4,512]{2,1,0:T(4,128)S(1)}, s32[24,4,512]{2,1,0:T(4,128)}, u32[]{:S(2)}) copy-start(s32[24,4,512]{2,1,0:T(4,128)} %param.25) | copy-start | bytes 589828
  17.0 5.0 %copy-start.14 = (f32[32,2]{0,1:T(2,128)S(1)}, f32[32,2]{0,1:T(2,128)}, u32[]{:S(2)}) copy-start(f32[32,2]{0,1:T(2,128)} %param.30) | copy-start | bytes 772
  24.0 3.1 copy-start.1
  32.1 175.8 %all-gather.10.cloned.1.call-start = ((), (), s32[]{:S(2)}) async-start(), calls=%async_computation.2 | async-start | bytes 3538944 | tf_op jit(solution)/shard_map/all_gather | solution.py:120
  58.4 104.7 %copy-start.5 = (bf16[128,1024]{1,0:T(8,128)(2,1)S(1)}, bf16[128,1024]{1,0:T(8,128)(2,1)}, u32[]{:S(2)}) copy-start(bf16[128,1024]{1,0:T(8,128)(2,1)} %param.31) | copy-start | bytes 786436
  84.8 79.4 %copy-start.7 = (s32[4,24,2]{1,2,0:T(2,128)S(1)}, s32[4,24,2]{1,2,0:T(2,128)}, u32[]{:S(2)}) copy-start(s32[4,24,2]{1,2,0:T(2,128)} %param.37) | copy-start | bytes 2308
  163.0 47.2 %copy-start.13 = (f32[1024]{0:T(1024)S(1)}, f32[1024]{0:T(1024)}, u32[]{:S(2)}) copy-start(f32[1024]{0:T(1024)} %param.32) | copy-start | bytes 12292
  164.1 137.1 %reduce-scatter.4.cloned.1.call-start = ((), (), s32[]{:S(2)}) async-start(), calls=%async_computation.3 | async-start | bytes 540672
  207.9 4.2 copy-start.3
  210.1 1.8 copy-start.4
  375.6 6.8 %copy-start.8 = (f32[1024]{0:T(1024)S(1)}, f32[1024]{0:T(1024)}, u32[]{:S(2)}) copy-start(f32[1024]{0:T(1024)} %param.38) | copy-start | bytes 12292
  382.4 66.1 %copy-start.6 = (bf16[12,1024]{1,0:T(8,128)(2,1)}, bf16[12,1024]{1,0:T(8,128)(2,1)S(1)}, u32[]{:S(2)}) copy-start(bf16[12,1024]{1,0:T(8,128)(2,1)S(1)} %get-tuple-element.243) | copy-start | bytes 73732
  382.4 66.1 %copy-start.9 = (f32[12]{0:T(128)}, f32[12]{0:T(128)S(1)}, u32[]{:S(2)}) copy-start(f32[12]{0:T(128)S(1)} %add_sqrt_fusion) | copy-start | bytes 148
Sparse Core Ops, SparseCore 0:
  32.2 53.4 all-gather.7
  164.3 43.5 all-gather.9
  217.0 84.2 reduce-scatter.3
